TPU v7x, 32 devices: a whole 2x2x4 slice. The times are simulated.
32 devices in a mesh: dp: 8 (over y, x, core), rep: 4 (over z).
Axes of the slice: x: 2, y: 2, z: 4, core: 2. Of those that a mesh axis runs over, the one named last changes fastest.
Arguments:
- tokens: bfloat16 [4096, 2048], P(('dp', 'rep')), may hold values from -6 to 6
- cotangent: bfloat16 [4096, 2048], P(('dp', 'rep')), may hold values from -0.125 to 0.125
- doc_ids: int32 [64, 64], P(('dp', 'rep')), may hold values from 0 to 3, never falling along the last dimension, each value on 1 to 32 neighbouring positions
- valid_len: int32 [64], P(('dp', 'rep')), may hold values from 16 to 64
- w_qkv: bfloat16 [2048, 384], P('dp'), may hold values from -0.125 to 0.125
- w_out: bfloat16 [2048, 128], P('dp'), may hold values from -0.5 to 0.5
- norm_gain: bfloat16 [2048], P('dp'), may hold values from 0.5 to 1.5
Outputs:
- grad_qkv: float32 [2048, 384], P('dp')
- grad_out: float32 [2048, 128], P('dp')
- grad_gain: float32 [2048], P('dp')
Inputs may be any that keep to these rules, and one draw needn't show every extreme that they name: `doc_ids`: within each row of 64 positions the ids never fall, and a document has 1 to 32 positions.
All inputs are finite; a program needn't handle non-finite values.
Results may differ from a plain program's by a relative error of at most 0.0079.
Values may be sent and summed in bfloat16 or wider, within the bound.
A program may use at most 64 MiB of HBM per device.

v0:
```python
import math

import jax
import jax.numpy as jnp
from jax import lax
from jax.sharding import PartitionSpec as P

NORM_EPS = 1e-06
ROPE_BASE = 1000000.0


def rotate(vector):
    half_size = vector.shape[-1] // 2
    return jnp.concatenate([-vector[..., half_size:], vector[..., :half_size]], axis=-1)


def unrotate(vector):
    half_size = vector.shape[-1] // 2
    return jnp.concatenate([vector[..., half_size:], -vector[..., :half_size]], axis=-1)


def tables(doc_rows, head_size):
    seq_length = doc_rows.shape[1]
    earlier = jnp.sum((doc_rows[:, None, :] < doc_rows[:, :, None]).astype(jnp.int32), axis=2)
    offsets = (jnp.arange(seq_length, dtype=jnp.int32)[None, :] - earlier).astype(jnp.float32)
    frequency = ROPE_BASE ** (-2.0 * jnp.arange(head_size // 2, dtype=jnp.float32) / head_size)
    angles = offsets[:, :, None] * frequency
    angles = jnp.concatenate([angles, angles], axis=2)
    return (jnp.cos(angles), jnp.sin(angles))


def forward_pass(inputs, doc_rows, w_qkv_full, gain_full):
    batches, seq_length, model_width = inputs.shape
    head_size = w_qkv_full.shape[1] // 3
    scale = 1.0 / math.sqrt(head_size)
    wide_in = inputs.astype(jnp.float32)
    inverse_rms = lax.rsqrt(jnp.mean(wide_in * wide_in, axis=2, keepdims=True) + NORM_EPS)
    scaled_in = wide_in * inverse_rms
    normed = (scaled_in * gain_full.astype(jnp.float32)).astype(jnp.bfloat16)
    projected = jnp.dot(
        normed.reshape(-1, model_width), w_qkv_full, preferred_element_type=jnp.float32
    )
    projected = projected.reshape(batches, seq_length, 3 * head_size)
    cosine, sine_part = tables(doc_rows, head_size)
    queries = projected[:, :, :head_size]
    keys_raw = projected[:, :, head_size : 2 * head_size]
    values_raw = projected[:, :, 2 * head_size :]
    query_rot = ((queries * cosine + rotate(queries) * sine_part) * scale).astype(jnp.bfloat16)
    key_rot = (keys_raw * cosine + rotate(keys_raw) * sine_part).astype(jnp.bfloat16)
    values = values_raw.astype(jnp.bfloat16)
    scores = jnp.einsum("msh,mth->mst", query_rot, key_rot, preferred_element_type=jnp.float32)
    order_row = jnp.arange(seq_length, dtype=jnp.int32)[:, None]
    order_col = jnp.arange(seq_length, dtype=jnp.int32)[None, :]
    allowed = (doc_rows[:, :, None] == doc_rows[:, None, :]) & (order_col <= order_row)[None]
    raised = jnp.where(allowed, jnp.exp(scores), 0.0)
    probabilities = raised / jnp.sum(raised, axis=2, keepdims=True)
    probs_low = probabilities.astype(jnp.bfloat16)
    attended = jnp.einsum(
        "mst,mth->msh", probs_low, values, preferred_element_type=jnp.float32
    ).astype(jnp.bfloat16)
    return (
        scaled_in,
        normed,
        query_rot,
        key_rot,
        values,
        probabilities,
        probs_low,
        attended,
        cosine,
        sine_part,
    )


def backward_pass(saved, live_dy, w_qkv_full, w_out_full):
    (
        scaled_in,
        normed,
        query_rot,
        key_rot,
        values,
        probabilities,
        probs_low,
        attended,
        cosine,
        sine_part,
    ) = saved
    batches, seq_length, model_width = live_dy.shape
    head_size = w_out_full.shape[1]
    scale = 1.0 / math.sqrt(head_size)
    d_attended = jnp.dot(
        live_dy.reshape(-1, model_width), w_out_full, preferred_element_type=jnp.float32
    )
    d_attended = d_attended.reshape(batches, seq_length, head_size).astype(jnp.bfloat16)
    d_probs = jnp.einsum("msh,mth->mst", d_attended, values, preferred_element_type=jnp.float32)
    d_values = jnp.einsum("mst,msh->mth", probs_low, d_attended, preferred_element_type=jnp.float32)
    d_scores = (
        probabilities * (d_probs - jnp.sum(probabilities * d_probs, axis=2, keepdims=True))
    ).astype(jnp.bfloat16)
    d_query = (
        jnp.einsum("mst,mth->msh", d_scores, key_rot, preferred_element_type=jnp.float32) * scale
    )
    d_key = jnp.einsum("mst,msh->mth", d_scores, query_rot, preferred_element_type=jnp.float32)
    d_query = d_query * cosine + unrotate(d_query * sine_part)
    d_key = d_key * cosine + unrotate(d_key * sine_part)
    d_qkv = jnp.concatenate([d_query, d_key, d_values], axis=2).astype(jnp.bfloat16)
    d_normed = lax.dot_general(
        d_qkv.reshape(-1, 3 * head_size),
        w_qkv_full,
        (((1,), (1,)), ((), ())),
        preferred_element_type=jnp.float32,
    )
    gain_term = jnp.sum(d_normed * scaled_in.reshape(-1, model_width), axis=0)
    return (d_qkv, gain_term)


def shards(tokens, cotangent, doc_ids, valid_len, w_qkv, w_out, norm_gain):
    batches, seq_length = doc_ids.shape
    model_width = tokens.shape[1]
    inputs = tokens.reshape(batches, seq_length, model_width)
    live_rows = jnp.arange(seq_length, dtype=jnp.int32)[None, :] < valid_len[:, None]
    live_dy = jnp.where(
        live_rows[:, :, None],
        cotangent.reshape(batches, seq_length, model_width),
        jnp.zeros((), jnp.bfloat16),
    )
    full_set = (
        lax.all_gather(w_qkv, "dp", axis=0, tiled=True),
        lax.all_gather(w_out, "dp", axis=0, tiled=True),
        lax.all_gather(norm_gain, "dp", axis=0, tiled=True),
    )
    saved = forward_pass(inputs, doc_ids, full_set[0], full_set[2])
    qkv_all, gain_total = backward_pass(saved, live_dy, full_set[0], full_set[1])
    normed_all = saved[1]
    attended_all = saved[7]
    head_size = w_out.shape[1]
    normed_flat = normed_all.reshape(-1, model_width)
    qkv_flat = qkv_all.reshape(-1, 3 * head_size)
    attended_flat = attended_all.reshape(-1, head_size)
    grad_qkv = lax.dot_general(
        normed_flat, qkv_flat, (((0,), (0,)), ((), ())), preferred_element_type=jnp.float32
    )
    grad_out = lax.dot_general(
        live_dy.reshape(-1, model_width),
        attended_flat,
        (((0,), (0,)), ((), ())),
        preferred_element_type=jnp.float32,
    )
    shares = (
        lax.psum_scatter(grad_qkv, "dp", scatter_dimension=0, tiled=True),
        lax.psum_scatter(grad_out, "dp", scatter_dimension=0, tiled=True),
    )
    shares = lax.psum((shares[0], shares[1]), "rep")
    gain_whole = lax.psum(gain_total, ("dp", "rep"))
    owned_rows = w_qkv.shape[0]
    gain_start = lax.axis_index("dp") * owned_rows
    gain_owned = lax.dynamic_slice_in_dim(gain_whole, gain_start, owned_rows, 0)
    replicas = lax.axis_size("rep")
    return (shares[0] / replicas, shares[1] / replicas, gain_owned / replicas)


def solution(mesh):
    in_specs = (
        P(("dp", "rep"), None),
        P(("dp", "rep"), None),
        P(("dp", "rep"), None),
        P(("dp", "rep")),
        P("dp", None),
        P("dp", None),
        P("dp"),
    )
    out_specs = (P("dp", None), P("dp", None), P("dp"))
    return jax.shard_map(shards, mesh=mesh, in_specs=in_specs, out_specs=out_specs, check_vma=False)
```

profile of v0, /device:TPU:0, one launch (start us, length us, event | category | flops | bytes accessed | tf_op | source)
XLA Modules:
  0.0 179.0 jit_solution(12147938299542766601)
XLA Ops:
  7.2 0.7 all-gather.3.cloned.1.call-update
  8.0 0.7 iota_compare_fusion.1
  8.7 0.1 lt.34
  8.8 1.3 multiply_reduce_fusion
  10.1 0.1 rsqrt.13
  10.2 0.7 reshape.109
  10.8 10.4 %all-gather = bf16[8,1,256]{2,1,0:T(2,128)(2,1)S(1)} all-gather(bf16[1,1,256]{2,1,0:T(2,128)(2,1)S(1)} %reshape.109), channel_id=1, replica_groups=mesh['dp'=8,'rep'=4] {'dp'}, dimensions={0}, use_global_device_ids=true | all-gather | bytes 4608 | tf_op jit(solution)/shard_map/all_gather | solution.py:130
  21.3 0.8 convert_reduce_fusion
  22.1 9.8 %all_gather.11 = bf16[2048,128]{1,0:T(8,128)(2,1)S(1)} all-gather(bf16[256,128]{1,0:T(8,128)(2,1)} %param.12), channel_id=1, replica_groups=mesh['dp'=8,'rep'=4] {'dp'}, dimensions={0}, use_global_device_ids=true | all-gather | bytes 589824 | tf_op jit(solution)/shard_map/all_gather | solution.py:129
  32.1 0.1 broadcast_select_fusion
  32.2 0.3 convolution_convert_fusion.2
  32.5 0.2 multiply_convert_fusion
  32.7 5.5 %all-gather.3.cloned.1.call-done = bf16[2048,384]{1,0:T(8,128)(2,1)} async-done(((bf16[256,384]{1,0:T(8,128)(2,1)}), bf16[2048,384]{1,0:T(8,128)(2,1)}) %all-gather.3.cloned.1.call-update) | async-done | bytes 1572880 | tf_op jit(solution)/shard_map/all_gather | solution.py:128
  38.2 1.9 %fusion = f32[2,64,384]{2,1,0:T(8,128)S(1)} fusion(bf16[2,64,2048]{2,1,0:T(8,128)(2,1)S(1)} %bitcast.33, bf16[2048,384]{1,0:T(8,128)(2,1)} %all-gather.3.cloned.1.call-done), kind=kOutput, calls=%fused_computation.3 | convolution fusion | flops 201326592 | bytes 2293760 | tf_op jit(solution)/shard_map/dot_general | solution.py:40
  40.1 0.1 slice_negate_fusion.2
  40.2 0.1 fusion.36
  40.3 0.3 fusion.21
  40.7 0.2 multiply_reduce_fusion.1
  40.8 1.5 convolution_bitcast_fusion.1
  42.4 0.3 fusion.32
  42.8 0.3 fusion.25
  43.3 0.3 fusion.26
  43.6 0.1 convolution_convert_fusion.1
  43.7 2.3 %convolution_bitcast_fusion = f32[2048,384]{1,0:T(8,128)} fusion(f32[2048]{0:T(1024)S(1)} %bitcast.38, f32[2,64]{1,0:T(2,128)S(1)} %rsqrt.13, bf16[2,64,128]{2,1,0:T(8,128)(2,1)S(1)} %convolution_convert_fusion.1, bf16[2,64,128]{2,1,0:T(8,128)(2,1)S(1)} %fusion.26, bf16[2,64,128]{2,1,0:T(8,128)(2,1)S(1)} %get-tuple-element.11, ...), kind=kOutput, calls=%fused_computation | convolution fusion | flops 202670080 | bytes 3777024 | tf_op jit(solution)/shard_map/dot_general | solution.py:140
  46.1 32.4 %reduce-scatter.5.cloned.1.call-done = f32[256,128]{1,0:T(8,128)} async-done(((f32[2048,128]{1,0:T(8,128)}), f32[256,128]{1,0:T(8,128)}) %reduce-scatter.5.cloned.1.call-update) | async-done | bytes 131088 | tf_op jit(solution)/shard_map/reduce_scatter | solution.py:151
  78.5 49.5 %reduce-scatter.3.cloned.1.call-done = f32[256,384]{1,0:T(8,128)} async-done(((f32[2048,384]{1,0:T(8,128)}), f32[256,384]{1,0:T(8,128)}) %reduce-scatter.3.cloned.1.call-update) | async-done | bytes 393232 | tf_op jit(solution)/shard_map/reduce_scatter | solution.py:150
  128.0 0.6 fusion.2
  128.7 39.5 %psum.23 = f32[2048]{0:T(1024)S(1)} all-reduce(f32[2048]{0:T(1024)S(1)} %fusion.2), channel_id=1, replica_groups=mesh['dp'=8,'rep'=4] {'dp','rep'}, use_global_device_ids=true, to_apply=%region_9.10 | all-reduce | flops 2048 | bytes 16384 | tf_op jit(solution)/shard_map/psum | solution.py:154
  168.2 0.6 dynamic-slice_multiply_fusion
  168.8 0.4 all-reduce.3.cloned.1.call-done
  169.2 1.8 broadcast_multiply_fusion
  170.9 1.6 broadcast_multiply_fusion.1
  (24 shorter events, 0.5 us)
Async XLA Ops:
  7.2 24.9 %copy-start.1 = (bf16[128,2048]{1,0:T(8,128)(2,1)S(1)}, bf16[128,2048]{1,0:T(8,128)(2,1)}, u32[]{:S(2)}) copy-start(bf16[128,2048]{1,0:T(8,128)(2,1)} %param.8) | copy-start | bytes 1572868
  7.2 31.0 %all-gather.3.cloned.1.call-start = ((), (), s32[]{:S(2)}) async-start(), calls=%async_computation.2 | async-start | bytes 1769472 | tf_op jit(solution)/shard_map/all_gather | solution.py:128
  7.9 70.6 %reduce-scatter.5.cloned.1.call-start = ((), (), s32[]{:S(2)}) async-start(), calls=%async_computation.4 | async-start | bytes 1179648 | tf_op jit(solution)/shard_map/reduce_scatter | solution.py:151
  8.8 23.7 %copy-start = (bf16[128,2048]{1,0:T(8,128)(2,1)S(1)}, bf16[128,2048]{1,0:T(8,128)(2,1)}, u32[]{:S(2)}) copy-start(bf16[128,2048]{1,0:T(8,128)(2,1)} %param.7) | copy-start | bytes 1572868
  38.2 2.5 %copy-start.3 = (s32[2,64]{1,0:T(2,128)S(1)}, s32[2,64]{1,0:T(2,128)}, u32[]{:S(2)}) copy-start(s32[2,64]{1,0:T(2,128)} %param.9) | copy-start | bytes 1540
  42.4 85.6 %reduce-scatter.3.cloned.1.call-start = ((), (), s32[]{:S(2)}) async-start(), calls=%async_computation.3 | async-start | bytes 3538944 | tf_op jit(solution)/shard_map/reduce_scatter | solution.py:150
  46.0 82.0 %copy-start.2 = (bf16[2048,384]{1,0:T(8,128)(2,1)S(1)}, bf16[2048,384]{1,0:T(8,128)(2,1)}, u32[]{:S(2)}) copy-start(bf16[2048,384]{1,0:T(8,128)(2,1)} %all-gather.3.cloned.1.call-done) | copy-start | bytes 4718596
  46.1 123.1 %all-reduce.3.cloned.1.call-start = ((), (), s32[]{:S(2)}) async-start(), calls=%async_computation.5 | async-start | bytes 1048576 | tf_op jit(solution)/shard_map/psum | solution.py:153
Sparse Core Ops, SparseCore 0:
  9.9 28.2 all-gather.2
  42.5 35.9 reduce-scatter.4
  81.9 46.0 reduce-scatter.2
  130.3 38.8 all-reduce.2
where the time goes:
time: 179 us
  waiting for transfers between devices  88.5 us (49%)
  blocking collectives  59.7 us (33%)
  between operations  13.9 us (8%)
  other arithmetic  8.19 us (5%)
  matrix products  7.7 us (4%)
    reduce_scatter x1, waiting for transfers between devices, shards(): lax.psum_scatter(grad_qkv, 'dp', scatter_dimension=0, tiled=True)  49.5 us
    psum x1, blocking collectives, shards(): gain_whole = lax.psum(gain_total, ('dp', 'rep'))  39.5 us
    reduce_scatter x1, waiting for transfers between devices, shards(): lax.psum_scatter(grad_out, 'dp', scatter_dimension=0, tiled=True)  32.4 us
    all_gather x1, blocking collectives, shards(): lax.all_gather(norm_gain, 'dp', axis=0, tiled=True)  10.4 us
    all_gather x1, blocking collectives, shards(): lax.all_gather(w_out, 'dp', axis=0, tiled=True)  9.83 us
    all_gather x1, waiting for transfers between devices, shards(): lax.all_gather(w_qkv, 'dp', axis=0, tiled=True)  5.52 us
    div x3, other arithmetic, shards(): return (shares[0] / replicas, shares[1] / replicas, gain_owned / replicas)  3.97 us
  transfers between devices with their start and end apart: 4, of which 4 were waited for; matrix products, arithmetic and copies ran while one was open for 5% of the time, Pallas kernels for 0%

commit v1 on v0

--- a/solution.py
+++ b/solution.py
@@ -1,8 +1,11 @@
+import functools
 import math
 
 import jax
 import jax.numpy as jnp
 from jax import lax
+from jax.experimental import pallas as pl
+from jax.experimental.pallas import tpu as pltpu
 from jax.sharding import PartitionSpec as P
 
 NORM_EPS = 1e-06
@@ -159,6 +162,360 @@
     return (shares[0] / replicas, shares[1] / replicas, gain_owned / replicas)
 
 
+MESH = pl.DeviceIdType.MESH
+LANES = 128
+CORES = 2
+
+
+def mm(left, right, dims):
+    return lax.dot_general(left, right, (dims, ((), ())), preferred_element_type=jnp.float32)
+
+
+def eye(size):
+    return lax.broadcasted_iota(jnp.int32, (size, size), 0) == lax.broadcasted_iota(
+        jnp.int32, (size, size), 1
+    )
+
+
+def to_column(row):
+    return jnp.sum(jnp.where(eye(row.shape[1]), row, 0.0), axis=1, keepdims=True)
+
+
+def to_row(column):
+    return jnp.sum(jnp.where(eye(column.shape[0]), column, 0.0), axis=0, keepdims=True)
+
+
+def fused(
+    n,
+    replicas,
+    x_ref,
+    dy_ref,
+    doc_ref,
+    valid_ref,
+    wq_ref,
+    wo_ref,
+    gain_ref,
+    gq_ref,
+    go_ref,
+    gg_ref,
+    w_all,
+    x_all,
+    dy_all,
+    y_all,
+    acc,
+    rs_send,
+    rs_recv,
+    g_all,
+    w_send_sem,
+    w_recv_sem,
+    a_send_sem,
+    a_recv_sem,
+    y_send_sem,
+    y_recv_sem,
+    r_send_sem,
+    r_recv_sem,
+    g_send_sem,
+    g_recv_sem,
+):
+    me = lax.axis_index("dp")
+    rep = lax.axis_index("rep")
+    chips = n // CORES
+    chip, core = me // CORES, lax.rem(me, CORES)
+    sibling = chip * CORES + (1 - core)
+    rows, width = x_ref.shape
+    owned = wq_ref.shape[0]
+    head = wo_ref.shape[1]
+    wide = 3 * head
+    samples, seq = doc_ref.shape
+    piece = owned // replicas
+    scale = 1.0 / math.sqrt(head)
+
+    barrier = pltpu.get_barrier_semaphore()
+    for off in range(1, n):
+        pl.semaphore_signal(
+            barrier, inc=1, device_id={"dp": lax.rem(me + off, n)}, device_id_type=MESH
+        )
+    for off in range(1, replicas):
+        pl.semaphore_signal(
+            barrier,
+            inc=1,
+            device_id={"rep": lax.rem(rep + off, replicas)},
+            device_id_type=MESH,
+        )
+
+    gain_col = to_column(gain_ref[...].astype(jnp.float32))
+    my_w = pl.ds(pl.multiple_of(me * owned, LANES), owned)
+    w_all[my_w, :wide] = (wq_ref[...].astype(jnp.float32) * gain_col).astype(jnp.bfloat16)
+    w_all[my_w, wide:] = wo_ref[...]
+
+    pl.semaphore_wait(barrier, n - 1 + replicas - 1)
+
+    pending = []
+
+    def send(src, dst, send_sem, recv_sem, where):
+        copy = pltpu.make_async_remote_copy(
+            src_ref=src,
+            dst_ref=dst,
+            send_sem=send_sem,
+            recv_sem=recv_sem,
+            device_id=where,
+            device_id_type=MESH,
+        )
+        copy.start()
+        pending.append(copy)
+        return copy
+
+    def origin(off, other):
+        lane = 1 - core if other else core
+        return lax.rem(chip + chips - off, chips) * CORES + lane
+
+    def spread(buf, block, send_sem, recv_sem):
+        mine = buf.at[pl.ds(pl.multiple_of(me * block, LANES), block)]
+        direct = {}
+        for off in range(1, chips):
+            peer = lax.rem(chip + off, chips) * CORES + core
+            direct[off] = send(mine, mine, send_sem.at[off], recv_sem.at[off], {"dp": peer})
+        passed = {
+            0: send(mine, mine, send_sem.at[chips], recv_sem.at[chips], {"dp": sibling})
+        }
+        return direct, passed
+
+    def hand_on(buf, block, off, direct, passed, send_sem, recv_sem):
+        direct[off].wait_recv()
+        got = buf.at[pl.ds(pl.multiple_of(origin(off, False) * block, LANES), block)]
+        passed[off] = send(
+            got, got, send_sem.at[chips + off], recv_sem.at[chips + off], {"dp": sibling}
+        )
+
+    direct, passed = spread(w_all, owned, w_send_sem, w_recv_sem)
+
+    wide_in = x_ref[...].astype(jnp.float32)
+    inverse = lax.rsqrt(
+        jnp.sum(wide_in * wide_in, axis=1, keepdims=True) * (1.0 / width) + NORM_EPS
+    )
+    keys, live = [], []
+    for m in range(samples):
+        doc_row = doc_ref[m : m + 1, :].astype(jnp.float32)
+        keys.append(to_column(doc_row) + float(m * seq))
+        place = lax.broadcasted_iota(jnp.int32, (seq, 1), 0)
+        live.append(jnp.where(place < valid_ref[m], 1.0, 0.0))
+    key_col = jnp.concatenate(keys, axis=0)
+    live_col = jnp.concatenate(live, axis=0)
+    key_row = to_row(key_col)
+    earlier = jnp.sum(jnp.where(key_row < key_col, 1.0, 0.0), axis=1, keepdims=True)
+    order_row = lax.broadcasted_iota(jnp.int32, (rows, rows), 0)
+    order_col = lax.broadcasted_iota(jnp.int32, (rows, rows), 1)
+    allowed = (key_row == key_col) & (order_col <= order_row)
+    offsets = lax.broadcasted_iota(jnp.int32, (rows, 1), 0).astype(jnp.float32) - earlier
+    lane = lax.broadcasted_iota(jnp.int32, (1, head), 1)
+    half = lax.rem(lane, head // 2).astype(jnp.float32)
+    frequency = jnp.exp(half * (-2.0 / head * math.log(ROPE_BASE)))
+    angles = offsets * frequency
+    cosine = jnp.cos(angles)
+    signed = jnp.sin(angles) * jnp.where(lane < head // 2, -1.0, 1.0)
+
+    def times(source, total):
+        cols = pl.ds(pl.multiple_of(source * owned, LANES), owned)
+        projected = mm(x_ref[:, cols], w_all[cols, :wide], ((1,), (0,)))
+        d_att = mm(dy_ref[:, cols], w_all[cols, wide:], ((1,), (0,)))
+        if total is None:
+            return projected, d_att
+        return total[0] + projected, total[1] + d_att
+
+    total = times(me, None)
+    passed[0].wait_recv()
+    total = times(sibling, total)
+    for off in range(1, chips):
+        hand_on(w_all, owned, off, direct, passed, w_send_sem, w_recv_sem)
+        total = times(origin(off, False), total)
+
+    my_rows = pl.ds(pl.multiple_of(me * rows, LANES), rows)
+    columns = {}
+    for off in range(1, n):
+        peer = lax.rem(me + off, n)
+        cols = pl.ds(pl.multiple_of(peer * owned, LANES), owned)
+        columns[off] = (
+            send(
+                x_ref.at[:, cols],
+                x_all.at[my_rows],
+                a_send_sem.at[0, off],
+                a_recv_sem.at[0, off],
+                {"dp": peer},
+            ),
+            send(
+                dy_ref.at[:, cols],
+                dy_all.at[my_rows],
+                a_send_sem.at[1, off],
+                a_recv_sem.at[1, off],
+                {"dp": peer},
+            ),
+        )
+
+    for off in range(1, chips):
+        passed[off].wait_recv()
+        total = times(origin(off, True), total)
+
+    projected = total[0] * inverse
+    d_att = (total[1] * live_col).astype(jnp.bfloat16)
+
+    def turn(vector, sine_part):
+        return vector * cosine + pltpu.roll(vector, head // 2, 1) * sine_part
+
+    query = (turn(projected[:, :head], signed) * scale).astype(jnp.bfloat16)
+    key = turn(projected[:, head : 2 * head], signed).astype(jnp.bfloat16)
+    values = projected[:, 2 * head :].astype(jnp.bfloat16)
+    scores = mm(query, key, ((1,), (1,)))
+    raised = jnp.where(allowed, jnp.exp(scores), 0.0)
+    probs = raised / jnp.sum(raised, axis=1, keepdims=True)
+    probs_low = probs.astype(jnp.bfloat16)
+    attended = mm(probs_low, values, ((1,), (0,)))
+    d_probs = mm(d_att, values, ((1,), (1,)))
+    d_values = mm(probs_low, d_att, ((0,), (0,)))
+    d_scores = (
+        probs * (d_probs - jnp.sum(probs * d_probs, axis=1, keepdims=True))
+    ).astype(jnp.bfloat16)
+    d_query = turn(mm(d_scores, key, ((1,), (0,))) * scale, -signed)
+    d_key = turn(mm(d_scores, query, ((0,), (0,))), -signed)
+    y_all[my_rows, :head] = (d_query * inverse).astype(jnp.bfloat16)
+    y_all[my_rows, head : 2 * head] = (d_key * inverse).astype(jnp.bfloat16)
+    y_all[my_rows, 2 * head : wide] = (d_values * inverse).astype(jnp.bfloat16)
+    y_all[my_rows, wide:] = (attended * live_col).astype(jnp.bfloat16)
+
+    direct, passed = spread(y_all, rows, y_send_sem, y_recv_sem)
+
+    my_cols = pl.ds(pl.multiple_of(me * owned, LANES), owned)
+    acc[:, :wide] = mm(x_ref[:, my_cols], y_all[my_rows, :wide], ((0,), (0,)))
+    acc[:, wide:] = mm(dy_ref[:, my_cols], y_all[my_rows, wide:], ((0,), (0,)))
+    for off in range(1, n):
+        for copy in columns[off]:
+            copy.wait_recv()
+
+    def gather(source):
+        part = pl.ds(pl.multiple_of(source * rows, LANES), rows)
+        acc[:, :wide] += mm(x_all[part, :], y_all[part, :wide], ((0,), (0,)))
+        acc[:, wide:] += mm(dy_all[part, :], y_all[part, wide:], ((0,), (0,)))
+
+    passed[0].wait_recv()
+    gather(sibling)
+    for off in range(1, chips):
+        hand_on(y_all, rows, off, direct, passed, y_send_sem, y_recv_sem)
+        gather(origin(off, False))
+    for off in range(1, chips):
+        passed[off].wait_recv()
+        gather(origin(off, True))
+
+    rs_send[...] = acc[...].astype(jnp.bfloat16)
+    sums = []
+    for off in range(1, replicas):
+        peer = lax.rem(rep + off, replicas)
+        part = pl.ds(pl.multiple_of(peer * piece, 16), piece)
+        sums.append(
+            send(
+                rs_send.at[part],
+                rs_recv.at[off - 1],
+                r_send_sem.at[off],
+                r_recv_sem.at[off],
+                {"rep": peer},
+            )
+        )
+    mine = pl.ds(pl.multiple_of(rep * piece, 16), piece)
+    whole = acc[mine, :]
+    for off in range(1, replicas):
+        sums[off - 1].wait_recv()
+        whole = whole + rs_recv[off - 1].astype(jnp.float32)
+    g_all[mine, :] = (whole * (1.0 / replicas)).astype(jnp.bfloat16)
+    last = []
+    for off in range(1, replicas):
+        peer = lax.rem(rep + off, replicas)
+        last.append(
+            send(
+                g_all.at[mine],
+                g_all.at[mine],
+                g_send_sem.at[off],
+                g_recv_sem.at[off],
+                {"rep": peer},
+            )
+        )
+    for copy in last:
+        copy.wait_recv()
+    total_q = g_all[:, :wide].astype(jnp.float32)
+    gq_ref[...] = total_q * gain_col
+    go_ref[...] = g_all[:, wide:].astype(jnp.float32)
+    gg_ref[...] = to_row(
+        jnp.sum(total_q * wq_ref[...].astype(jnp.float32), axis=1, keepdims=True)
+    )
+    for copy in pending:
+        copy.wait_send()
+
+
+def one_kernel(n, replicas, tokens, cotangent, doc_ids, valid_len, w_qkv, w_out, norm_gain):
+    rows, width = tokens.shape
+    owned, wide = w_qkv.shape
+    head = w_out.shape[1]
+    chips = n // CORES
+    vmem = pl.BlockSpec(memory_space=pltpu.VMEM)
+    smem = pl.BlockSpec(memory_space=pltpu.SMEM)
+    low = jnp.bfloat16
+    full = wide + head
+    sem = pltpu.SemaphoreType.DMA
+    grad_qkv, grad_out, grad_gain = pl.pallas_call(
+        functools.partial(fused, n, replicas),
+        out_shape=(
+            jax.ShapeDtypeStruct((owned, wide), jnp.float32),
+            jax.ShapeDtypeStruct((owned, head), jnp.float32),
+            jax.ShapeDtypeStruct((1, owned), jnp.float32),
+        ),
+        in_specs=[vmem, vmem, vmem, smem, vmem, vmem, vmem],
+        out_specs=(vmem, vmem, vmem),
+        scratch_shapes=[
+            pltpu.VMEM((width, full), low),
+            pltpu.VMEM((n * rows, owned), low),
+            pltpu.VMEM((n * rows, owned), low),
+            pltpu.VMEM((n * rows, full), low),
+            pltpu.VMEM((owned, full), jnp.float32),
+            pltpu.VMEM((owned, full), low),
+            pltpu.VMEM((replicas - 1, owned // replicas, full), low),
+            pltpu.VMEM((owned, full), low),
+            sem((2 * chips,)),
+            sem((2 * chips,)),
+            sem((2, n)),
+            sem((2, n)),
+            sem((2 * chips,)),
+            sem((2 * chips,)),
+            sem((replicas,)),
+            sem((replicas,)),
+            sem((replicas,)),
+            sem((replicas,)),
+        ],
+        compiler_params=pltpu.CompilerParams(
+            collective_id=0, has_side_effects=True, vmem_limit_bytes=48 * 1024 * 1024
+        ),
+    )(tokens, cotangent, doc_ids, valid_len, w_qkv, w_out, norm_gain.reshape(1, owned))
+    return grad_qkv, grad_out, grad_gain.reshape(owned)
+
+
+def shards_or_kernel(
+    n, replicas, tokens, cotangent, doc_ids, valid_len, w_qkv, w_out, norm_gain
+):
+    rows, owned, head = tokens.shape[0], w_qkv.shape[0], w_out.shape[1]
+    fits = (
+        n % CORES == 0
+        and n > CORES
+        and replicas > 1
+        and owned % LANES == 0
+        and owned % (16 * replicas) == 0
+        and rows % LANES == 0
+        and rows * n <= 2048
+        and head == LANES
+        and doc_ids.shape[1] % 8 == 0
+    )
+    if not fits:
+        return shards(tokens, cotangent, doc_ids, valid_len, w_qkv, w_out, norm_gain)
+    return one_kernel(
+        n, replicas, tokens, cotangent, doc_ids, valid_len, w_qkv, w_out, norm_gain
+    )
+
+
 def solution(mesh):
     in_specs = (
         P(("dp", "rep"), None),
@@ -170,4 +527,5 @@
         P("dp"),
     )
     out_specs = (P("dp", None), P("dp", None), P("dp"))
-    return jax.shard_map(shards, mesh=mesh, in_specs=in_specs, out_specs=out_specs, check_vma=False)
+    body = functools.partial(shards_or_kernel, mesh.shape["dp"], mesh.shape["rep"])
+    return jax.shard_map(body, mesh=mesh, in_specs=in_specs, out_specs=out_specs, check_vma=False)

time: 179 us -> 61.5 us (0.34)
  waiting for transfers between devices: 88.5 us -> 0 us
  blocking collectives: 59.7 us -> 0 us
  Pallas kernels: 0 us -> 54 us
  between operations: 13.9 us -> 0.66 us
  other arithmetic: 8.19 us -> 0 us
  matrix products: 7.7 us -> 0 us
  local copies, waits for them, and re-layouts: 0.85 us -> 6.49 us
    reduce_scatter x2 -> x0, waiting for transfers between devices: 81.9 us -> none  [the longest x1 49.5 us: shards(): lax.psum_scatter(grad_qkv, 'dp', scatter_dimension=0, tiled=True)]
    pallas_call x0 -> x1, Pallas kernels: none -> 54 us  [one_kernel(): pl.pallas_call(functools.partial(fused, n, replicas), out_shape=(jax.Shap...]
    psum x1 -> x0, blocking collectives: 39.5 us -> none  [shards(): gain_whole = lax.psum(gain_total, ('dp', 'rep'))]
    all_gather x2 -> x0, blocking collectives: 20.2 us -> none  [the longest x1 10.4 us: shards(): lax.all_gather(norm_gain, 'dp', axis=0, tiled=True)]
    dot_general x9 -> x0, matrix products: 7.51 us -> none  [the longest x1 2.35 us: shards(): lax.dot_general(normed_flat, qkv_flat, (((0,), (0,)), ((), ())), preferre...]
    all_gather x1 -> x0, waiting for transfers between devices: 5.52 us -> none  [shards(): lax.all_gather(w_qkv, 'dp', axis=0, tiled=True)]
    unnamed x9 -> x15, local copies, waits for them, and re-layouts: 0.68 us -> 5.82 us
    div x3 -> x0, other arithmetic: 3.97 us -> none  [shards(): return (shares[0] / replicas, shares[1] / replicas, gain_owned / replicas)]
  transfers between devices with their start and end apart: 4 -> 0, of which waited for: 4 -> 0; matrix products, arithmetic and copies ran while one was open for 5% -> 0% of each run, Pallas kernels for 0% -> 0%
where the time goes in v1:
time: 61.5 us; the launch traced here: 61.2 us
  Pallas kernels  54 us (88%)
  local copies, waits for them, and re-layouts  6.49 us (11%)
  between operations  0.66 us (1%)
    pallas_call x1, Pallas kernels, one_kernel(): pl.pallas_call(functools.partial(fused, n, replicas), out_shape=(jax.Shap...  54 us
    unnamed x15, local copies, waits for them, and re-layouts  5.82 us

profile of v1, /device:TPU:0, one launch (start us, length us, event | category | flops | bytes accessed | tf_op | source)
XLA Modules:
  0.0 61.2 jit_solution(13229505871730450052)
XLA Ops:
  0.6 0.0 copy-start.5
  0.6 0.0 copy-start.4
  0.7 0.7 %reshape.12.gain_ref = bf16[1,256]{1,0:T(2,128)(2,1)S(1)} reshape(bf16[256]{0:T(256)(128)(2,1)} %param.13) | data formatting | bytes 1024 | tf_op jit(solution)/shard_map/reshape | solution.py:493
  1.3 0.0 copy-done.5
  1.3 0.0 copy-done.4
  1.3 0.0 copy-start
  1.3 1.0 %copy-done = bf16[128,2048]{1,0:T(8,128)(2,1)S(1)} copy-done((bf16[128,2048]{1,0:T(8,128)(2,1)S(1)}, bf16[128,2048]{1,0:T(8,128)(2,1)}, u32[]{:S(2)}) %copy-start) | copy-done | bytes 524312
  2.4 0.0 copy-start.1
  2.4 1.0 %copy-done.1 = bf16[128,2048]{1,0:T(8,128)(2,1)S(1)} copy-done((bf16[128,2048]{1,0:T(8,128)(2,1)S(1)}, bf16[128,2048]{1,0:T(8,128)(2,1)}, u32[]{:S(2)}) %copy-start.1) | copy-done | bytes 524312
  3.4 0.0 copy-start.2
  3.4 0.9 %copy-done.2 = bf16[256,384]{1,0:T(8,128)(2,1)S(1)} copy-done((bf16[256,384]{1,0:T(8,128)(2,1)S(1)}, bf16[256,384]{1,0:T(8,128)(2,1)}, u32[]{:S(2)}) %copy-start.2) | copy-done | bytes 196632
  4.3 0.0 copy-start.3
  4.3 0.8 %copy-done.3 = bf16[256,128]{1,0:T(8,128)(2,1)S(1)} copy-done((bf16[256,128]{1,0:T(8,128)(2,1)S(1)}, bf16[256,128]{1,0:T(8,128)(2,1)}, u32[]{:S(2)}) %copy-start.3) | copy-done | bytes 65560
  5.2 54.0 %shard_map.94 = (f32[256,384]{1,0:T(8,128)S(1)}, f32[256,128]{1,0:T(8,128)S(1)}, f32[1,256]{1,0:T(1,128)S(1)}) custom-call(bf16[128,2048]{1,0:T(8,128)(2,1)S(1)} %copy-done, bf16[128,2048]{1,0:T(8,128)(2,1)S(1)} %copy-done.1, s32[2,64]{1,0:T(2,128)S(1)} %copy-done.4, s32[2]{0:T(128)S(1)} %copy-done.5, bf16[256,384]{1,0:T(8,128)(2,1)S(1)} %copy-done.2, ...), custom_call_target="tpu_custom_call" | custom-call | tf_op jit(solution)/shard_map/pallas_call | solution.py:461
  59.2 0.7 %copy.13 = f32[256,384]{1,0:T(8,128)} copy(f32[256,384]{1,0:T(8,128)S(1)} %get-tuple-element.12) | data formatting | bytes 786432
  60.0 0.7 %copy.14 = f32[256,128]{1,0:T(8,128)} copy(f32[256,128]{1,0:T(8,128)S(1)} %get-tuple-element.13) | data formatting | bytes 262144
  60.6 0.6 copy.15
Async XLA Ops:
  0.6 0.7 %copy-start.5 = (s32[2]{0:T(128)S(1)}, s32[2]{0:T(128)}, u32[]{:S(2)}) copy-start(s32[2]{0:T(128)} %valid_ref.1) | copy-start | bytes 28
  0.6 0.7 %copy-start.4 = (s32[2,64]{1,0:T(2,128)S(1)}, s32[2,64]{1,0:T(2,128)}, u32[]{:S(2)}) copy-start(s32[2,64]{1,0:T(2,128)} %doc_ref.1) | copy-start | bytes 1540
  1.3 1.0 %copy-start = (bf16[128,2048]{1,0:T(8,128)(2,1)S(1)}, bf16[128,2048]{1,0:T(8,128)(2,1)}, u32[]{:S(2)}) copy-start(bf16[128,2048]{1,0:T(8,128)(2,1)} %x_ref.1) | copy-start | bytes 1572868
  2.4 1.0 %copy-start.1 = (bf16[128,2048]{1,0:T(8,128)(2,1)S(1)}, bf16[128,2048]{1,0:T(8,128)(2,1)}, u32[]{:S(2)}) copy-start(bf16[128,2048]{1,0:T(8,128)(2,1)} %dy_ref.1) | copy-start | bytes 1572868
  3.4 0.9 %copy-start.2 = (bf16[256,384]{1,0:T(8,128)(2,1)S(1)}, bf16[256,384]{1,0:T(8,128)(2,1)}, u32[]{:S(2)}) copy-start(bf16[256,384]{1,0:T(8,128)(2,1)} %wq_ref.1) | copy-start | bytes 589828
  4.3 0.8 %copy-start.3 = (bf16[256,128]{1,0:T(8,128)(2,1)S(1)}, bf16[256,128]{1,0:T(8,128)(2,1)}, u32[]{:S(2)}) copy-start(bf16[256,128]{1,0:T(8,128)(2,1)} %wo_ref.1) | copy-start | bytes 196612

commit v2 on v1

--- a/solution.py
+++ b/solution.py
@@ -1,4 +1,5 @@
 import functools
+import itertools
 import math
 
 import jax
@@ -199,6 +200,7 @@
     go_ref,
     gg_ref,
     w_all,
+    gain_all,
     x_all,
     dy_all,
     y_all,
@@ -208,6 +210,8 @@
     g_all,
     w_send_sem,
     w_recv_sem,
+    s_send_sem,
+    s_recv_sem,
     a_send_sem,
     a_recv_sem,
     y_send_sem,
@@ -219,7 +223,6 @@
 ):
     me = lax.axis_index("dp")
     rep = lax.axis_index("rep")
-    chips = n // CORES
     chip, core = me // CORES, lax.rem(me, CORES)
     sibling = chip * CORES + (1 - core)
     rows, width = x_ref.shape
@@ -243,9 +246,11 @@
             device_id_type=MESH,
         )
 
-    gain_col = to_column(gain_ref[...].astype(jnp.float32))
+    gain_row = gain_ref[...].astype(jnp.float32)
+    gain_col = to_column(gain_row)
+    gain_all[me] = jnp.broadcast_to(gain_row, gain_all.shape[1:])
     my_w = pl.ds(pl.multiple_of(me * owned, LANES), owned)
-    w_all[my_w, :wide] = (wq_ref[...].astype(jnp.float32) * gain_col).astype(jnp.bfloat16)
+    w_all[my_w, :wide] = wq_ref[...]
     w_all[my_w, wide:] = wo_ref[...]
 
     pl.semaphore_wait(barrier, n - 1 + replicas - 1)
@@ -265,29 +270,67 @@
         pending.append(copy)
         return copy
 
-    def origin(off, other):
-        lane = 1 - core if other else core
-        return lax.rem(chip + chips - off, chips) * CORES + lane
+    along, across = lax.rem(chip, 2), chip // 2
+    by_x = across * 2 + 1 - along
+    by_y = (1 - across) * 2 + along
+    first = by_x + core * (by_y - by_x)
+    second = by_y + core * (by_x - by_y)
+    far = 3 - chip
+    owners = (
+        first * CORES + core,
+        second * CORES + core,
+        far * CORES + core,
+        sibling,
+        second * CORES + 1 - core,
+        first * CORES + 1 - core,
+        far * CORES + 1 - core,
+    )
 
     def spread(buf, block, send_sem, recv_sem):
+        def part(slot):
+            start = pl.multiple_of(owners[slot] * block, LANES)
+            return buf.at[pl.ds(start, block)]
+
+        def copy(source, slot, device):
+            return send(
+                source, source, send_sem.at[slot], recv_sem.at[slot], {"dp": device}
+            )
+
         mine = buf.at[pl.ds(pl.multiple_of(me * block, LANES), block)]
-        direct = {}
-        for off in range(1, chips):
-            peer = lax.rem(chip + off, chips) * CORES + core
-            direct[off] = send(mine, mine, send_sem.at[off], recv_sem.at[off], {"dp": peer})
-        passed = {
-            0: send(mine, mine, send_sem.at[chips], recv_sem.at[chips], {"dp": sibling})
-        }
-        return direct, passed
-
-    def hand_on(buf, block, off, direct, passed, send_sem, recv_sem):
-        direct[off].wait_recv()
-        got = buf.at[pl.ds(pl.multiple_of(origin(off, False) * block, LANES), block)]
-        passed[off] = send(
-            got, got, send_sem.at[chips + off], recv_sem.at[chips + off], {"dp": sibling}
-        )
-
-    direct, passed = spread(w_all, owned, w_send_sem, w_recv_sem)
+        straight = copy(mine, 0, owners[0])
+        straight_second = copy(mine, 1, owners[1])
+        passed = copy(mine, 3, sibling)
+        yield None
+        passed.wait_recv()
+        yield owners[3]
+        straight.wait_recv()
+        relayed = copy(part(0), 2, owners[1])
+        passed_first = copy(part(0), 4, sibling)
+        yield owners[0]
+        straight_second.wait_recv()
+        passed_second = copy(part(1), 5, sibling)
+        yield owners[1]
+        passed_first.wait_recv()
+        yield owners[4]
+        passed_second.wait_recv()
+        yield owners[5]
+        relayed.wait_recv()
+        passed_far = copy(part(2), 6, sibling)
+        yield owners[2]
+        passed_far.wait_recv()
+        yield owners[6]
+
+    arrivals = spread(w_all, owned, w_send_sem, w_recv_sem)
+    next(arrivals)
+    gains = {}
+    for off in range(1, n):
+        gains[off] = send(
+            gain_all.at[me],
+            gain_all.at[me],
+            s_send_sem.at[off],
+            s_recv_sem.at[off],
+            {"dp": lax.rem(me + off, n)},
+        )
 
     wide_in = x_ref[...].astype(jnp.float32)
     inverse = lax.rsqrt(
@@ -316,18 +359,19 @@
 
     def times(source, total):
         cols = pl.ds(pl.multiple_of(source * owned, LANES), owned)
-        projected = mm(x_ref[:, cols], w_all[cols, :wide], ((1,), (0,)))
+        scaled = x_ref[:, cols].astype(jnp.float32) * inverse
+        normed = (scaled * gain_all[source][0:1]).astype(jnp.bfloat16)
+        projected = mm(normed, w_all[cols, :wide], ((1,), (0,)))
         d_att = mm(dy_ref[:, cols], w_all[cols, wide:], ((1,), (0,)))
         if total is None:
             return projected, d_att
         return total[0] + projected, total[1] + d_att
 
     total = times(me, None)
-    passed[0].wait_recv()
-    total = times(sibling, total)
-    for off in range(1, chips):
-        hand_on(w_all, owned, off, direct, passed, w_send_sem, w_recv_sem)
-        total = times(origin(off, False), total)
+    for off in range(1, n):
+        gains[off].wait_recv()
+    for source in itertools.islice(arrivals, n - 2):
+        total = times(source, total)
 
     my_rows = pl.ds(pl.multiple_of(me * rows, LANES), rows)
     columns = {}
@@ -351,11 +395,10 @@
             ),
         )
 
-    for off in range(1, chips):
-        passed[off].wait_recv()
-        total = times(origin(off, True), total)
-
-    projected = total[0] * inverse
+    for source in arrivals:
+        total = times(source, total)
+
+    projected = total[0]
     d_att = (total[1] * live_col).astype(jnp.bfloat16)
 
     def turn(vector, sine_part):
@@ -381,7 +424,8 @@
     y_all[my_rows, 2 * head : wide] = (d_values * inverse).astype(jnp.bfloat16)
     y_all[my_rows, wide:] = (attended * live_col).astype(jnp.bfloat16)
 
-    direct, passed = spread(y_all, rows, y_send_sem, y_recv_sem)
+    arrivals = spread(y_all, rows, y_send_sem, y_recv_sem)
+    next(arrivals)
 
     my_cols = pl.ds(pl.multiple_of(me * owned, LANES), owned)
     acc[:, :wide] = mm(x_ref[:, my_cols], y_all[my_rows, :wide], ((0,), (0,)))
@@ -395,14 +439,8 @@
         acc[:, :wide] += mm(x_all[part, :], y_all[part, :wide], ((0,), (0,)))
         acc[:, wide:] += mm(dy_all[part, :], y_all[part, wide:], ((0,), (0,)))
 
-    passed[0].wait_recv()
-    gather(sibling)
-    for off in range(1, chips):
-        hand_on(y_all, rows, off, direct, passed, y_send_sem, y_recv_sem)
-        gather(origin(off, False))
-    for off in range(1, chips):
-        passed[off].wait_recv()
-        gather(origin(off, True))
+    for source in arrivals:
+        gather(source)
 
     rs_send[...] = acc[...].astype(jnp.bfloat16)
     sums = []
@@ -452,7 +490,6 @@
     rows, width = tokens.shape
     owned, wide = w_qkv.shape
     head = w_out.shape[1]
-    chips = n // CORES
     vmem = pl.BlockSpec(memory_space=pltpu.VMEM)
     smem = pl.BlockSpec(memory_space=pltpu.SMEM)
     low = jnp.bfloat16
@@ -469,6 +506,7 @@
         out_specs=(vmem, vmem, vmem),
         scratch_shapes=[
             pltpu.VMEM((width, full), low),
+            pltpu.VMEM((n, 8, owned), jnp.float32),
             pltpu.VMEM((n * rows, owned), low),
             pltpu.VMEM((n * rows, owned), low),
             pltpu.VMEM((n * rows, full), low),
@@ -476,12 +514,14 @@
             pltpu.VMEM((owned, full), low),
             pltpu.VMEM((replicas - 1, owned // replicas, full), low),
             pltpu.VMEM((owned, full), low),
-            sem((2 * chips,)),
-            sem((2 * chips,)),
+            sem((n - 1,)),
+            sem((n - 1,)),
+            sem((n,)),
+            sem((n,)),
             sem((2, n)),
             sem((2, n)),
-            sem((2 * chips,)),
-            sem((2 * chips,)),
+            sem((n - 1,)),
+            sem((n - 1,)),
             sem((replicas,)),
             sem((replicas,)),
             sem((replicas,)),
@@ -499,8 +539,7 @@
 ):
     rows, owned, head = tokens.shape[0], w_qkv.shape[0], w_out.shape[1]
     fits = (
-        n % CORES == 0
-        and n > CORES
+        n == 4 * CORES
         and replicas > 1
         and owned % LANES == 0
         and owned % (16 * replicas) == 0

time: 61.5 us -> 61.4 us (level)
  no operation moved by 1% of the time
where the time goes in v2:
time: 61.4 us; the launch traced here: 61.1 us
  Pallas kernels  54 us (88%)
  local copies, waits for them, and re-layouts  6.49 us (11%)
  between operations  0.66 us (1%)
    pallas_call x1, Pallas kernels, one_kernel(): pl.pallas_call(functools.partial(fused, n, replicas), out_shape=(jax.Shap...  54 us
    unnamed x15, local copies, waits for them, and re-layouts  5.82 us

profile of v2, /device:TPU:0, one launch (start us, length us, event | category | flops | bytes accessed | tf_op | source)
XLA Modules:
  0.0 61.1 jit_solution(1820005208150617346)
XLA Ops:
  0.6 0.0 copy-start.5
  0.6 0.0 copy-start.4
  0.7 0.7 %reshape.12.gain_ref = bf16[1,256]{1,0:T(2,128)(2,1)S(1)} reshape(bf16[256]{0:T(256)(128)(2,1)} %param.13) | data formatting | bytes 1024 | tf_op jit(solution)/shard_map/reshape | solution.py:533
  1.3 0.0 copy-done.5
  1.3 0.0 copy-done.4
  1.3 0.0 copy-start
  1.3 1.0 %copy-done = bf16[128,2048]{1,0:T(8,128)(2,1)S(1)} copy-done((bf16[128,2048]{1,0:T(8,128)(2,1)S(1)}, bf16[128,2048]{1,0:T(8,128)(2,1)}, u32[]{:S(2)}) %copy-start) | copy-done | bytes 524312
  2.4 0.0 copy-start.1
  2.4 1.0 %copy-done.1 = bf16[128,2048]{1,0:T(8,128)(2,1)S(1)} copy-done((bf16[128,2048]{1,0:T(8,128)(2,1)S(1)}, bf16[128,2048]{1,0:T(8,128)(2,1)}, u32[]{:S(2)}) %copy-start.1) | copy-done | bytes 524312
  3.4 0.0 copy-start.2
  3.4 0.9 %copy-done.2 = bf16[256,384]{1,0:T(8,128)(2,1)S(1)} copy-done((bf16[256,384]{1,0:T(8,128)(2,1)S(1)}, bf16[256,384]{1,0:T(8,128)(2,1)}, u32[]{:S(2)}) %copy-start.2) | copy-done | bytes 196632
  4.3 0.0 copy-start.3
  4.3 0.8 %copy-done.3 = bf16[256,128]{1,0:T(8,128)(2,1)S(1)} copy-done((bf16[256,128]{1,0:T(8,128)(2,1)S(1)}, bf16[256,128]{1,0:T(8,128)(2,1)}, u32[]{:S(2)}) %copy-start.3) | copy-done | bytes 65560
  5.2 54.0 %shard_map.94 = (f32[256,384]{1,0:T(8,128)S(1)}, f32[256,128]{1,0:T(8,128)S(1)}, f32[1,256]{1,0:T(1,128)S(1)}) custom-call(bf16[128,2048]{1,0:T(8,128)(2,1)S(1)} %copy-done, bf16[128,2048]{1,0:T(8,128)(2,1)S(1)} %copy-done.1, s32[2,64]{1,0:T(2,128)S(1)} %copy-done.4, s32[2]{0:T(128)S(1)} %copy-done.5, bf16[256,384]{1,0:T(8,128)(2,1)S(1)} %copy-done.2, ...), custom_call_target="tpu_custom_call" | custom-call | tf_op jit(solution)/shard_map/pallas_call | solution.py:498
  59.2 0.7 %copy.13 = f32[256,384]{1,0:T(8,128)} copy(f32[256,384]{1,0:T(8,128)S(1)} %get-tuple-element.12) | data formatting | bytes 786432
  59.9 0.7 %copy.14 = f32[256,128]{1,0:T(8,128)} copy(f32[256,128]{1,0:T(8,128)S(1)} %get-tuple-element.13) | data formatting | bytes 262144
  60.6 0.6 copy.15
Async XLA Ops:
  0.6 0.7 %copy-start.5 = (s32[2]{0:T(128)S(1)}, s32[2]{0:T(128)}, u32[]{:S(2)}) copy-start(s32[2]{0:T(128)} %valid_ref.1) | copy-start | bytes 28
  0.6 0.7 %copy-start.4 = (s32[2,64]{1,0:T(2,128)S(1)}, s32[2,64]{1,0:T(2,128)}, u32[]{:S(2)}) copy-start(s32[2,64]{1,0:T(2,128)} %doc_ref.1) | copy-start | bytes 1540
  1.3 1.0 %copy-start = (bf16[128,2048]{1,0:T(8,128)(2,1)S(1)}, bf16[128,2048]{1,0:T(8,128)(2,1)}, u32[]{:S(2)}) copy-start(bf16[128,2048]{1,0:T(8,128)(2,1)} %x_ref.1) | copy-start | bytes 1572868
  2.4 1.0 %copy-start.1 = (bf16[128,2048]{1,0:T(8,128)(2,1)S(1)}, bf16[128,2048]{1,0:T(8,128)(2,1)}, u32[]{:S(2)}) copy-start(bf16[128,2048]{1,0:T(8,128)(2,1)} %dy_ref.1) | copy-start | bytes 1572868
  3.4 0.9 %copy-start.2 = (bf16[256,384]{1,0:T(8,128)(2,1)S(1)}, bf16[256,384]{1,0:T(8,128)(2,1)}, u32[]{:S(2)}) copy-start(bf16[256,384]{1,0:T(8,128)(2,1)} %wq_ref.1) | copy-start | bytes 589828
  4.3 0.8 %copy-start.3 = (bf16[256,128]{1,0:T(8,128)(2,1)S(1)}, bf16[256,128]{1,0:T(8,128)(2,1)}, u32[]{:S(2)}) copy-start(bf16[256,128]{1,0:T(8,128)(2,1)} %wo_ref.1) | copy-start | bytes 196612

commit v3 on v2

--- a/solution.py
+++ b/solution.py
@@ -189,16 +189,19 @@
 def fused(
     n,
     replicas,
-    x_ref,
-    dy_ref,
+    x_hbm,
+    dy_hbm,
     doc_ref,
     valid_ref,
-    wq_ref,
-    wo_ref,
+    wq_hbm,
+    wo_hbm,
     gain_ref,
     gq_ref,
     go_ref,
     gg_ref,
+    x_ref,
+    dy_ref,
+    in_sem,
     w_all,
     gain_all,
     x_all,
@@ -226,12 +229,22 @@
     chip, core = me // CORES, lax.rem(me, CORES)
     sibling = chip * CORES + (1 - core)
     rows, width = x_ref.shape
-    owned = wq_ref.shape[0]
-    head = wo_ref.shape[1]
+    owned = wq_hbm.shape[0]
+    head = wo_hbm.shape[1]
     wide = 3 * head
     samples, seq = doc_ref.shape
     piece = owned // replicas
     scale = 1.0 / math.sqrt(head)
+
+    my_w = pl.ds(pl.multiple_of(me * owned, LANES), owned)
+    loads = (
+        pltpu.make_async_copy(wq_hbm, w_all.at[my_w, pl.ds(0, wide)], in_sem.at[0]),
+        pltpu.make_async_copy(wo_hbm, w_all.at[my_w, pl.ds(wide, head)], in_sem.at[1]),
+        pltpu.make_async_copy(x_hbm, x_ref, in_sem.at[2]),
+        pltpu.make_async_copy(dy_hbm, dy_ref, in_sem.at[3]),
+    )
+    for load in loads:
+        load.start()
 
     barrier = pltpu.get_barrier_semaphore()
     for off in range(1, n):
@@ -249,10 +262,8 @@
     gain_row = gain_ref[...].astype(jnp.float32)
     gain_col = to_column(gain_row)
     gain_all[me] = jnp.broadcast_to(gain_row, gain_all.shape[1:])
-    my_w = pl.ds(pl.multiple_of(me * owned, LANES), owned)
-    w_all[my_w, :wide] = wq_ref[...]
-    w_all[my_w, wide:] = wo_ref[...]
-
+    loads[0].wait()
+    loads[1].wait()
     pl.semaphore_wait(barrier, n - 1 + replicas - 1)
 
     pending = []
@@ -332,6 +343,8 @@
             {"dp": lax.rem(me + off, n)},
         )
 
+    loads[2].wait()
+    loads[3].wait()
     wide_in = x_ref[...].astype(jnp.float32)
     inverse = lax.rsqrt(
         jnp.sum(wide_in * wide_in, axis=1, keepdims=True) * (1.0 / width) + NORM_EPS
@@ -480,7 +493,7 @@
     gq_ref[...] = total_q * gain_col
     go_ref[...] = g_all[:, wide:].astype(jnp.float32)
     gg_ref[...] = to_row(
-        jnp.sum(total_q * wq_ref[...].astype(jnp.float32), axis=1, keepdims=True)
+        jnp.sum(total_q * w_all[my_w, :wide].astype(jnp.float32), axis=1, keepdims=True)
     )
     for copy in pending:
         copy.wait_send()
@@ -491,6 +504,7 @@
     owned, wide = w_qkv.shape
     head = w_out.shape[1]
     vmem = pl.BlockSpec(memory_space=pltpu.VMEM)
+    hbm = pl.BlockSpec(memory_space=pltpu.HBM)
     smem = pl.BlockSpec(memory_space=pltpu.SMEM)
     low = jnp.bfloat16
     full = wide + head
@@ -502,9 +516,12 @@
             jax.ShapeDtypeStruct((owned, head), jnp.float32),
             jax.ShapeDtypeStruct((1, owned), jnp.float32),
         ),
-        in_specs=[vmem, vmem, vmem, smem, vmem, vmem, vmem],
+        in_specs=[hbm, hbm, vmem, smem, hbm, hbm, vmem],
         out_specs=(vmem, vmem, vmem),
         scratch_shapes=[
+            pltpu.VMEM((rows, width), low),
+            pltpu.VMEM((rows, width), low),
+            sem((4,)),
             pltpu.VMEM((width, full), low),
             pltpu.VMEM((n, 8, owned), jnp.float32),
             pltpu.VMEM((n * rows, owned), low),

time: 61.4 us -> 61.6 us (level)
  no operation moved by 1% of the time
where the time goes in v3:
time: 61.6 us; the launch traced here: 61.3 us
  Pallas kernels  54.1 us (88%)
  local copies, waits for them, and re-layouts  6.49 us (11%)
  between operations  0.66 us (1%)
    pallas_call x1, Pallas kernels, one_kernel(): pl.pallas_call(functools.partial(fused, n, replicas), out_shape=(jax.Shap...  54.1 us
    unnamed x15, local copies, waits for them, and re-layouts  5.82 us

profile of v3, /device:TPU:0, one launch (start us, length us, event | category | flops | bytes accessed | tf_op | source)
XLA Modules:
  0.0 61.3 jit_solution(6656975036340899533)
XLA Ops:
  0.6 0.0 copy-start.5
  0.6 0.0 copy-start.4
  0.7 0.7 %reshape.12.gain_ref = bf16[1,256]{1,0:T(2,128)(2,1)S(1)} reshape(bf16[256]{0:T(256)(128)(2,1)} %param.13) | data formatting | bytes 1024 | tf_op jit(solution)/shard_map/reshape | solution.py:550
  1.3 0.0 copy-done.5
  1.3 0.0 copy-done.4
  1.3 0.0 copy-start
  1.3 1.0 %copy-done = bf16[128,2048]{1,0:T(8,128)(2,1)S(1)} copy-done((bf16[128,2048]{1,0:T(8,128)(2,1)S(1)}, bf16[128,2048]{1,0:T(8,128)(2,1)}, u32[]{:S(2)}) %copy-start) | copy-done | bytes 524312
  2.4 0.0 copy-start.1
  2.4 1.0 %copy-done.1 = bf16[128,2048]{1,0:T(8,128)(2,1)S(1)} copy-done((bf16[128,2048]{1,0:T(8,128)(2,1)S(1)}, bf16[128,2048]{1,0:T(8,128)(2,1)}, u32[]{:S(2)}) %copy-start.1) | copy-done | bytes 524312
  3.4 0.0 copy-start.2
  3.4 0.9 %copy-done.2 = bf16[256,384]{1,0:T(8,128)(2,1)S(1)} copy-done((bf16[256,384]{1,0:T(8,128)(2,1)S(1)}, bf16[256,384]{1,0:T(8,128)(2,1)}, u32[]{:S(2)}) %copy-start.2) | copy-done | bytes 196632
  4.3 0.0 copy-start.3
  4.3 0.8 %copy-done.3 = bf16[256,128]{1,0:T(8,128)(2,1)S(1)} copy-done((bf16[256,128]{1,0:T(8,128)(2,1)S(1)}, bf16[256,128]{1,0:T(8,128)(2,1)}, u32[]{:S(2)}) %copy-start.3) | copy-done | bytes 65560
  5.2 54.1 %shard_map.94 = (f32[256,384]{1,0:T(8,128)S(1)}, f32[256,128]{1,0:T(8,128)S(1)}, f32[1,256]{1,0:T(1,128)S(1)}) custom-call(bf16[128,2048]{1,0:T(8,128)(2,1)S(1)} %copy-done, bf16[128,2048]{1,0:T(8,128)(2,1)S(1)} %copy-done.1, s32[2,64]{1,0:T(2,128)S(1)} %copy-done.4, s32[2]{0:T(128)S(1)} %copy-done.5, bf16[256,384]{1,0:T(8,128)(2,1)S(1)} %copy-done.2, ...), custom_call_target="tpu_custom_call" | custom-call | tf_op jit(solution)/shard_map/pallas_call | solution.py:512
  59.3 0.7 %copy.13 = f32[256,384]{1,0:T(8,128)} copy(f32[256,384]{1,0:T(8,128)S(1)} %get-tuple-element.12) | data formatting | bytes 786432
  60.1 0.7 %copy.14 = f32[256,128]{1,0:T(8,128)} copy(f32[256,128]{1,0:T(8,128)S(1)} %get-tuple-element.13) | data formatting | bytes 262144
  60.7 0.6 copy.15
Async XLA Ops:
  0.6 0.7 %copy-start.5 = (s32[2]{0:T(128)S(1)}, s32[2]{0:T(128)}, u32[]{:S(2)}) copy-start(s32[2]{0:T(128)} %valid_ref.1) | copy-start | bytes 28
  0.6 0.7 %copy-start.4 = (s32[2,64]{1,0:T(2,128)S(1)}, s32[2,64]{1,0:T(2,128)}, u32[]{:S(2)}) copy-start(s32[2,64]{1,0:T(2,128)} %doc_ref.1) | copy-start | bytes 1540
  1.3 1.0 %copy-start = (bf16[128,2048]{1,0:T(8,128)(2,1)S(1)}, bf16[128,2048]{1,0:T(8,128)(2,1)}, u32[]{:S(2)}) copy-start(bf16[128,2048]{1,0:T(8,128)(2,1)} %x_hbm.1) | copy-start | bytes 1572868
  2.4 1.0 %copy-start.1 = (bf16[128,2048]{1,0:T(8,128)(2,1)S(1)}, bf16[128,2048]{1,0:T(8,128)(2,1)}, u32[]{:S(2)}) copy-start(bf16[128,2048]{1,0:T(8,128)(2,1)} %dy_hbm.1) | copy-start | bytes 1572868
  3.4 0.9 %copy-start.2 = (bf16[256,384]{1,0:T(8,128)(2,1)S(1)}, bf16[256,384]{1,0:T(8,128)(2,1)}, u32[]{:S(2)}) copy-start(bf16[256,384]{1,0:T(8,128)(2,1)} %wq_hbm.1) | copy-start | bytes 589828
  4.3 0.8 %copy-start.3 = (bf16[256,128]{1,0:T(8,128)(2,1)S(1)}, bf16[256,128]{1,0:T(8,128)(2,1)}, u32[]{:S(2)}) copy-start(bf16[256,128]{1,0:T(8,128)(2,1)} %wo_hbm.1) | copy-start | bytes 196612
